TPU v7x, 256 devices: a whole 4x4x8 slice. The times are simulated.
256 devices in a mesh: gz: 2 (over core), row: 4 (over x), col: 32 (over z, y).
Axes of the slice: x: 4, y: 4, z: 8, core: 2. Of those that a mesh axis runs over, the one named last changes fastest.
Arguments:
- ancestor: float32 [4096, 16384], P('row', 'col'), may hold values from -6 to 6
- lower_panel: bfloat16 [2, 64, 24, 128, 128], P('gz', 'col', 'row'), may hold values from -6 to 6
- row_ids: int32 [2, 64, 24], P('gz', 'col', 'row'), may hold values from 0 to 7, as said below
- row_counts: int32 [2, 64, 4], P('gz', 'col', 'row'), may hold values from 1 to 6
- diag_inverse: bfloat16 [2, 64, 128, 128], P('gz', 'col'), may hold values from -0.5 to 0.5
- upper_panel: bfloat16 [2, 64, 96, 128, 128], P('gz', 'row', 'col'), may hold values from -0.1875 to 0.1875
- col_ids: int32 [2, 64, 96], P('gz', 'row', 'col'), may hold values from 0 to 3, as said below
- col_counts: int32 [2, 64, 32], P('gz', 'row', 'col'), may hold values from 1 to 3
Outputs:
- updated: float32 [4096, 16384], P('row', 'col')
Inputs may be any that keep to these rules, and one draw needn't show every extreme that they name: `row_ids`: within each layer, supernode and process row the 6 slots name distinct local block rows. `col_ids`: within each layer, supernode and process column the 3 slots name distinct local block columns.
All inputs are finite; a program needn't handle non-finite values.
Results may differ from a plain program's by a relative error of at most 0.0026.
Values may be sent and summed in bfloat16 or wider, within the bound.
A program may use at most 128 MiB of HBM per device.

v0:
```python
import jax
import jax.numpy as jnp
from jax import lax
from jax.sharding import PartitionSpec as P


def spread_rows(tiles, ids, counts, blocks):
    slots = ids.shape[1]
    slot_index = jnp.arange(slots, dtype=jnp.int32)
    alive = slot_index[None, :] < counts
    target = jnp.arange(blocks, dtype=jnp.int32)
    select = ((ids[:, :, None] == target[None, None, :]) & alive[:, :, None]).astype(jnp.bfloat16)
    dense = jnp.einsum("krl,krab->lakb", select, tiles, preferred_element_type=jnp.float32).astype(
        jnp.bfloat16
    )
    width = tiles.shape[-1]
    return dense.reshape(blocks * width, tiles.shape[0] * width)


def spread_cols(tiles, ids, counts, blocks):
    slots = ids.shape[1]
    slot_index = jnp.arange(slots, dtype=jnp.int32)
    alive = slot_index[None, :] < counts
    target = jnp.arange(blocks, dtype=jnp.int32)
    select = ((ids[:, :, None] == target[None, None, :]) & alive[:, :, None]).astype(jnp.bfloat16)
    dense = jnp.einsum("kcm,kcab->kamb", select, tiles, preferred_element_type=jnp.float32).astype(
        jnp.bfloat16
    )
    width = tiles.shape[-1]
    return dense.reshape(tiles.shape[0] * width, blocks * width)


def on_device(
    ancestor, lower_panel, row_ids, row_counts, diag_inverse, upper_panel, col_ids, col_counts
):
    width = lower_panel.shape[-1]
    row_blocks = ancestor.shape[0] // width
    col_blocks = ancestor.shape[1] // width
    solved = jnp.einsum(
        "ksab,kbc->ksac", lower_panel[0], diag_inverse[0], preferred_element_type=jnp.float32
    ).astype(jnp.bfloat16)
    piece = lax.all_gather((upper_panel[0], col_ids[0], col_counts[0]), "row", axis=0, tiled=True)
    upper_dense = spread_cols(piece[0], piece[1], piece[2], col_blocks)
    piece = lax.all_gather((solved, row_ids[0], row_counts[0]), "col", axis=0, tiled=True)
    lower_dense = spread_rows(piece[0], piece[1], piece[2], row_blocks)
    partial_sum = jnp.dot(lower_dense, upper_dense, preferred_element_type=jnp.float32)
    return ancestor - lax.psum(partial_sum, "gz")


def solution(mesh):
    placed = (
        P("row", "col"),
        P("gz", "col", "row", None, None),
        P("gz", "col", "row"),
        P("gz", "col", "row"),
        P("gz", "col", None, None),
        P("gz", "row", "col", None, None),
        P("gz", "row", "col"),
        P("gz", "row", "col"),
    )
    return jax.shard_map(
        on_device, mesh=mesh, in_specs=placed, out_specs=P("row", "col"), check_vma=False
    )
```

profile of v0, /device:TPU:1, one launch (start us, length us, event | category | flops | bytes accessed | tf_op | source)
XLA Modules:
  0.0 301.7 jit_solution(158132594757815860)
XLA Ops:
  6.5 0.0 copy-start
  6.5 0.0 all-gather.10.cloned.1.call-start
  6.5 0.7 all-gather.10.cloned.1.call-update
  7.3 0.0 all-gather.8.cloned.1.call-start
  7.3 0.2 copy-done
  7.5 1.8 convolution_convert_fusion
  9.4 0.0 all-gather.8.cloned.1.call-update
  9.4 0.0 all-reduce.4.cloned.1.call-start
  9.4 1.3 dynamic-slice
  10.8 1.3 dynamic-slice.1
  12.1 0.8 copy.17
  14.2 0.8 bitcast_dynamic-update-slice_fusion.1
  14.9 20.0 %all-reduce = s32[64]{0:T(128)S(1)} all-reduce(s32[64]{0:T(128)S(1)} %bitcast_dynamic-update-slice_fusion.1), channel_id=3, replica_groups=mesh['gz'=2,'row'=4,'col'=32] {'col'}, use_global_device_ids=true, to_apply=%add | all-reduce | flops 64 | bytes 512
  35.0 0.7 bitcast_dynamic-update-slice_fusion
  35.7 7.7 %all-reduce.1 = s32[64]{0:T(128)S(1)} all-reduce(s32[64]{0:T(128)S(1)} %bitcast_dynamic-update-slice_fusion), channel_id=5, replica_groups=mesh['gz'=2,'row'=4,'col'=32] {'row'}, use_global_device_ids=true, to_apply=%add.1 | all-reduce | flops 64 | bytes 512
  43.4 10.6 %all-gather.2 = s32[1,64,3]{2,0,1:T(1,128)S(1)} all-gather(s32[1,16,3]{2,0,1:T(1,128)S(1)} %copy.17), channel_id=4, replica_groups=mesh['gz'=2,'row'=4,'col'=32] {'row'}, dimensions={1}, use_global_device_ids=true | all-gather | bytes 960 | tf_op jit(solution)/shard_map/all_gather | solution.py:42
  54.0 35.0 %all-gather = s32[1,64,6]{2,0,1:T(1,128)S(1)} all-gather(s32[1,2,6]{2,0,1:T(1,128)} %bitcast.51), channel_id=2, replica_groups=mesh['gz'=2,'row'=4,'col'=32] {'col'}, dimensions={1}, use_global_device_ids=true | all-gather | bytes 1584 | tf_op jit(solution)/shard_map/all_gather | solution.py:44
  89.1 0.1 iota_compare_fusion.3
  89.1 0.1 iota_compare_fusion.2
  89.2 0.0 all-gather.10.cloned.1.call-done
  89.2 11.1 %fusion.12 = bf16[64,4,128,128]{3,1,2,0:T(4,128)(2,1)} fusion(bf16[1,64,3,128,128]{4,3,2,0,1:T(8,128)(2,1)} %all-gather.10.cloned.1.call-done, s32[64,3]{1,0:T(8,128)S(1)} %bitcast.50, pred[64,3]{1,0:T(8,128)(4,1)S(1)} %iota_compare_fusion.2), kind=kOutput, calls=%fused_computation.11 | convolution fusion | flops 29361664 | bytes 14681024 | tf_op jit(solution)/shard_map/kcm,kcab->kamb/dot_general | solution.py:26
  100.3 102.7 %all-gather.8.cloned.1.call-done = bf16[64,6,128,128]{3,2,1,0:T(8,128)(2,1)} async-done(((bf16[2,6,128,128]{3,2,1,0:T(8,128)(2,1)}), bf16[64,6,128,128]{3,2,1,0:T(8,128)(2,1)}) %all-gather.8.cloned.1.call-update) | async-done | bytes 12582928 | tf_op jit(solution)/shard_map/all_gather | solution.py:44
  203.0 16.6 %convert_bitcast_fusion = bf16[8,128,64,128]{3,0,1,2:T(8,128)(2,1)} fusion(bf16[64,6,128,128]{3,2,1,0:T(8,128)(2,1)} %all-gather.8.cloned.1.call-done, s32[64,6]{1,0:T(8,128)S(1)} %bitcast.49, pred[64,6]{1,0:T(8,128)(4,1)S(1)} %iota_compare_fusion.3), kind=kOutput, calls=%fused_computation.5 | convolution fusion | flops 109058048 | bytes 29362048 | tf_op jit(solution)/shard_map/krl,krab->lakb/dot_general | solution.py:13
  219.7 0.0 copy-start.3
  219.7 18.9 %copy.16 = bf16[8,128,64,128]{3,2,1,0:T(8,128)(2,1)} copy(bf16[8,128,64,128]{3,0,1,2:T(8,128)(2,1)} %convert_bitcast_fusion) | data formatting | bytes 33554432 | tf_op jit(solution)/shard_map/convert_element_type | solution.py:13
  238.6 0.0 copy-done.3
  238.6 0.0 copy-start.2
  238.6 0.0 copy-start.1
  238.6 22.4 %fusion = f32[1024,512]{1,0:T(8,128)} fusion(bf16[128,8,64,128]{3,2,1,0:T(8,128)(2,1)} %bitcast.47, bf16[1024,8,4,128]{3,2,1,0:T(4,128)(2,1)S(1)} %bitcast.52), kind=kOutput, calls=%fused_computation | convolution fusion | flops 8589934592 | bytes 27262976 | tf_op jit(solution)/shard_map/dot_general | solution.py:46
  261.0 0.0 all-reduce.4.cloned.1.call-update
  261.0 30.8 %all-reduce.4.cloned.1.call-done = f32[1024,512]{1,0:T(8,128)} async-done(((f32[1024,512]{1,0:T(8,128)}), f32[1024,512]{1,0:T(8,128)}) %all-reduce.4.cloned.1.call-update) | async-done | bytes 2097168 | tf_op jit(solution)/shard_map/psum | solution.py:47
  291.8 0.0 copy-done.2
  291.8 3.4 %sub.3 = f32[1024,512]{1,0:T(8,128)} subtract(f32[1024,512]{1,0:T(8,128)S(1)} %copy-done.2, f32[1024,512]{1,0:T(8,128)} %all-reduce.4.cloned.1.call-done) | non-fusion elementwise | flops 524288 | bytes 6291456 | tf_op jit(solution)/shard_map/sub | solution.py:47
  295.2 0.0 copy-done.1
  (2 shorter events, 0.0 us)
Async XLA Ops:
  6.5 1.0 copy-start
  6.5 82.7 %all-gather.10.cloned.1.call-start = ((), (), s32[]{:S(2)}) async-start(), calls=%async_computation.2 | async-start | bytes 7864320 | tf_op jit(solution)/shard_map/all_gather | solution.py:42
  7.3 195.8 %all-gather.8.cloned.1.call-start = ((), (), s32[]{:S(2)}) async-start(), calls=%async_computation | async-start | bytes 12976128 | tf_op jit(solution)/shard_map/all_gather | solution.py:44
  9.4 282.4 %all-reduce.4.cloned.1.call-start = ((), (), s32[]{:S(2)}) async-start(), calls=%async_computation.1 | async-start | bytes 4194304 | tf_op jit(solution)/shard_map/psum | solution.py:47
  219.7 18.9 %copy-start.3 = (bf16[64,4,128,128]{3,1,2,0:T(4,128)(2,1)S(1)}, bf16[64,4,128,128]{3,1,2,0:T(4,128)(2,1)}, u32[]{:S(2)}) copy-start(bf16[64,4,128,128]{3,1,2,0:T(4,128)(2,1)} %fusion.12) | copy-start | bytes 25165828
  238.6 53.2 %copy-start.2 = (f32[1024,512]{1,0:T(8,128)S(1)}, f32[1024,512]{1,0:T(8,128)}, u32[]{:S(2)}) copy-start(f32[1024,512]{1,0:T(8,128)} %param.8) | copy-start | bytes 6291460
  238.6 56.6 %copy-start.1 = (bf16[1,2,6,128,128]{4,3,2,1,0:T(8,128)(2,1)S(1)}, bf16[1,2,6,128,128]{4,3,2,1,0:T(8,128)(2,1)}, u32[]{:S(2)}) copy-start(bf16[1,2,6,128,128]{4,3,2,1,0:T(8,128)(2,1)} %param.9) | copy-start | bytes 1179652
Sparse Core Ops, SparseCore 0:
  9.1 72.1 all-gather.9
  83.9 119.0 all-gather.7
  261.1 30.5 all-reduce.3
where the time goes:
time: 302 us
  waiting for transfers between devices  134 us (44%)
  blocking collectives  73.4 us (24%)
  matrix products  52 us (17%)
  local copies, waits for them, and re-layouts  24.1 us (8%)
  between operations  14.5 us (5%)
  other arithmetic  3.53 us (1%)
    all_gather x1, waiting for transfers between devices, on_device(): lax.all_gather((solved, row_ids[0], row_counts[0]), 'col', axis=0, tiled=...  103 us
    all_gather x1, blocking collectives, on_device(): lax.all_gather((solved, row_ids[0], row_counts[0]), 'col', axis=0, tiled=...  35 us
    psum x1, waiting for transfers between devices, on_device(): return ancestor - lax.psum(partial_sum, 'gz')  30.8 us
    unnamed x2, blocking collectives  27.7 us
    dot_general x1, matrix products, on_device(): jnp.dot(lower_dense, upper_dense, preferred_element_type=jnp.float32)  22.4 us
    convert_element_type x1, local copies, waits for them, and re-layouts, spread_rows(): jnp.einsum('krl,krab->lakb', select, tiles, preferred_element_type=jnp.fl...  18.9 us
    dot_general x1, matrix products, spread_rows(): jnp.einsum('krl,krab->lakb', select, tiles, preferred_element_type=jnp.fl...  16.6 us
    dot_general x1, matrix products, spread_cols(): jnp.einsum('kcm,kcab->kamb', select, tiles, preferred_element_type=jnp.fl...  11.1 us
  transfers between devices with their start and end apart: 3, of which 2 were waited for; matrix products, arithmetic and copies ran while one was open for 6% of the time, Pallas kernels for 0%

commit v1 on v0

--- a/solution.py
+++ b/solution.py
@@ -44,7 +44,7 @@
     piece = lax.all_gather((solved, row_ids[0], row_counts[0]), "col", axis=0, tiled=True)
     lower_dense = spread_rows(piece[0], piece[1], piece[2], row_blocks)
     partial_sum = jnp.dot(lower_dense, upper_dense, preferred_element_type=jnp.float32)
-    return ancestor - lax.psum(partial_sum, "gz")
+    return ancestor - jnp.sum(lax.all_gather(partial_sum, "gz"), 0)
 
 
 def solution(mesh):

time: 302 us -> 292 us (0.967)
  waiting for transfers between devices: 134 us -> 121 us
    psum x1 -> x0, waiting for transfers between devices: 30.8 us -> none  [on_device(): return ancestor - lax.psum(partial_sum, 'gz')]
    all_gather x0 -> x1, waiting for transfers between devices: none -> 17.7 us  [on_device(): return ancestor - jnp.sum(lax.all_gather(partial_sum, 'gz'), 0)]
where the time goes in v1:
time: 292 us; the launch traced here: 291 us
  waiting for transfers between devices  121 us (41%)
  blocking collectives  73.4 us (25%)
  matrix products  51.8 us (18%)
  local copies, waits for them, and re-layouts  24 us (8%)
  between operations  14.4 us (5%)
  other arithmetic  6.39 us (2%)
    all_gather x1, waiting for transfers between devices, on_device(): lax.all_gather((solved, row_ids[0], row_counts[0]), 'col', axis=0, tiled=...  103 us
    all_gather x1, blocking collectives, on_device(): lax.all_gather((solved, row_ids[0], row_counts[0]), 'col', axis=0, tiled=...  35 us
    unnamed x2, blocking collectives  27.7 us
    dot_general x1, matrix products, on_device(): jnp.dot(lower_dense, upper_dense, preferred_element_type=jnp.float32)  22.3 us
    convert_element_type x1, local copies, waits for them, and re-layouts, spread_rows(): jnp.einsum('krl,krab->lakb', select, tiles, preferred_element_type=jnp.fl...  18.9 us
    all_gather x1, waiting for transfers between devices, on_device(): return ancestor - jnp.sum(lax.all_gather(partial_sum, 'gz'), 0)  17.7 us
    dot_general x1, matrix products, spread_rows(): jnp.einsum('krl,krab->lakb', select, tiles, preferred_element_type=jnp.fl...  16.6 us
    dot_general x1, matrix products, spread_cols(): jnp.einsum('kcm,kcab->kamb', select, tiles, preferred_element_type=jnp.fl...  11.1 us
  transfers between devices with their start and end apart: 3, of which 2 were waited for; matrix products, arithmetic and copies ran while one was open for 6% of the time, Pallas kernels for 0%

profile of v1, /device:TPU:1, one launch (start us, length us, event | category | flops | bytes accessed | tf_op | source)
XLA Modules:
  0.0 291.3 jit_solution(788987961180053190)
XLA Ops:
  6.5 0.0 copy-start
  6.5 0.0 all-gather.12.cloned.1.call-start
  6.5 0.7 all-gather.12.cloned.1.call-update
  7.3 0.0 all-gather.10.cloned.1.call-start
  7.3 0.2 copy-done
  7.5 1.8 convolution_convert_fusion
  9.4 0.0 all-gather.10.cloned.1.call-update
  9.4 0.0 all-gather.14.cloned.1.call-start
  9.4 1.3 dynamic-slice
  10.8 1.3 dynamic-slice.1
  12.0 0.8 copy.17
  14.1 0.8 bitcast_dynamic-update-slice_fusion.1
  14.8 20.0 %all-reduce = s32[64]{0:T(128)S(1)} all-reduce(s32[64]{0:T(128)S(1)} %bitcast_dynamic-update-slice_fusion.1), channel_id=3, replica_groups=mesh['gz'=2,'row'=4,'col'=32] {'col'}, use_global_device_ids=true, to_apply=%add | all-reduce | flops 64 | bytes 512
  34.8 0.7 bitcast_dynamic-update-slice_fusion
  35.6 7.7 %all-reduce.1 = s32[64]{0:T(128)S(1)} all-reduce(s32[64]{0:T(128)S(1)} %bitcast_dynamic-update-slice_fusion), channel_id=5, replica_groups=mesh['gz'=2,'row'=4,'col'=32] {'row'}, use_global_device_ids=true, to_apply=%add.1 | all-reduce | flops 64 | bytes 512
  43.3 10.6 %all-gather.2 = s32[1,64,3]{2,0,1:T(1,128)S(1)} all-gather(s32[1,16,3]{2,0,1:T(1,128)S(1)} %copy.17), channel_id=4, replica_groups=mesh['gz'=2,'row'=4,'col'=32] {'row'}, dimensions={1}, use_global_device_ids=true | all-gather | bytes 960 | tf_op jit(solution)/shard_map/all_gather | solution.py:42
  53.9 35.0 %all-gather = s32[1,64,6]{2,0,1:T(1,128)S(1)} all-gather(s32[1,2,6]{2,0,1:T(1,128)} %bitcast.53), channel_id=2, replica_groups=mesh['gz'=2,'row'=4,'col'=32] {'col'}, dimensions={1}, use_global_device_ids=true | all-gather | bytes 1584 | tf_op jit(solution)/shard_map/all_gather | solution.py:44
  88.9 0.1 iota_compare_fusion.3
  89.0 0.1 iota_compare_fusion.2
  89.1 0.0 all-gather.12.cloned.1.call-done
  89.1 11.1 %fusion.12 = bf16[64,4,128,128]{3,1,2,0:T(4,128)(2,1)} fusion(bf16[1,64,3,128,128]{4,3,2,0,1:T(8,128)(2,1)} %all-gather.12.cloned.1.call-done, s32[64,3]{1,0:T(8,128)S(1)} %bitcast.52, pred[64,3]{1,0:T(8,128)(4,1)S(1)} %iota_compare_fusion.2), kind=kOutput, calls=%fused_computation.11 | convolution fusion | flops 29361664 | bytes 14681024 | tf_op jit(solution)/shard_map/kcm,kcab->kamb/dot_general | solution.py:26
  100.2 102.8 %all-gather.10.cloned.1.call-done = bf16[64,6,128,128]{3,2,1,0:T(8,128)(2,1)} async-done(((bf16[2,6,128,128]{3,2,1,0:T(8,128)(2,1)}), bf16[64,6,128,128]{3,2,1,0:T(8,128)(2,1)}) %all-gather.10.cloned.1.call-update) | async-done | bytes 12582928 | tf_op jit(solution)/shard_map/all_gather | solution.py:44
  203.0 16.6 %convert_bitcast_fusion = bf16[8,128,64,128]{3,0,1,2:T(8,128)(2,1)} fusion(bf16[64,6,128,128]{3,2,1,0:T(8,128)(2,1)} %all-gather.10.cloned.1.call-done, s32[64,6]{1,0:T(8,128)S(1)} %bitcast.51, pred[64,6]{1,0:T(8,128)(4,1)S(1)} %iota_compare_fusion.3), kind=kOutput, calls=%fused_computation.5 | convolution fusion | flops 109058048 | bytes 29362048 | tf_op jit(solution)/shard_map/krl,krab->lakb/dot_general | solution.py:13
  219.7 0.0 copy-start.2
  219.7 18.9 %copy.16 = bf16[8,128,64,128]{3,2,1,0:T(8,128)(2,1)} copy(bf16[8,128,64,128]{3,0,1,2:T(8,128)(2,1)} %convert_bitcast_fusion) | data formatting | bytes 33554432 | tf_op jit(solution)/shard_map/convert_element_type | solution.py:13
  238.6 0.0 copy-done.2
  238.6 0.0 copy-start.1
  238.6 22.3 %fusion = f32[1024,512]{1,0:T(8,128)} fusion(bf16[128,8,64,128]{3,2,1,0:T(8,128)(2,1)} %bitcast.48, bf16[1024,8,4,128]{3,2,1,0:T(4,128)(2,1)S(1)} %bitcast.54), kind=kOutput, calls=%fused_computation | convolution fusion | flops 8589934592 | bytes 27262976 | tf_op jit(solution)/shard_map/dot_general | solution.py:46
  260.8 0.0 all-gather.14.cloned.1.call-update
  260.9 17.7 %all-gather.14.cloned.1.call-done = f32[2048,512]{1,0:T(8,128)} async-done(((f32[1024,512]{1,0:T(8,128)}), f32[2048,512]{1,0:T(8,128)}) %all-gather.14.cloned.1.call-update) | async-done | bytes 4194320 | tf_op jit(solution)/shard_map/all_gather | solution.py:47
  278.5 2.9 reduce_sum.9
  281.4 3.4 %sub.3 = f32[1024,512]{1,0:T(8,128)} subtract(f32[1024,512]{1,0:T(8,128)} %param.8, f32[1024,512]{1,0:T(8,128)S(1)} %reduce_sum.9) | non-fusion elementwise | flops 524288 | bytes 6291456 | tf_op jit(solution)/shard_map/sub | solution.py:47
  284.8 0.0 copy-done.1
  (2 shorter events, 0.0 us)
Async XLA Ops:
  6.5 1.0 copy-start
  6.5 82.6 %all-gather.12.cloned.1.call-start = ((), (), s32[]{:S(2)}) async-start(), calls=%async_computation.1 | async-start | bytes 7864320 | tf_op jit(solution)/shard_map/all_gather | solution.py:42
  7.3 195.8 %all-gather.10.cloned.1.call-start = ((), (), s32[]{:S(2)}) async-start(), calls=%async_computation | async-start | bytes 12976128 | tf_op jit(solution)/shard_map/all_gather | solution.py:44
  9.4 269.1 %all-gather.14.cloned.1.call-start = ((), (), s32[]{:S(2)}) async-start(), calls=%async_computation.2 | async-start | bytes 6291456 | tf_op jit(solution)/shard_map/all_gather | solution.py:47
  219.7 18.9 %copy-start.2 = (bf16[64,4,128,128]{3,1,2,0:T(4,128)(2,1)S(1)}, bf16[64,4,128,128]{3,1,2,0:T(4,128)(2,1)}, u32[]{:S(2)}) copy-start(bf16[64,4,128,128]{3,1,2,0:T(4,128)(2,1)} %fusion.12) | copy-start | bytes 25165828
  238.6 46.2 %copy-start.1 = (bf16[1,2,6,128,128]{4,3,2,1,0:T(8,128)(2,1)S(1)}, bf16[1,2,6,128,128]{4,3,2,1,0:T(8,128)(2,1)}, u32[]{:S(2)}) copy-start(bf16[1,2,6,128,128]{4,3,2,1,0:T(8,128)(2,1)} %param.9) | copy-start | bytes 1179652
Sparse Core Ops, SparseCore 0:
  9.1 72.1 all-gather.11
  83.9 119.0 all-gather.9
  261.0 17.5 all-gather.13
